TPU v7x, 32 devices: a whole 2x2x4 slice. The times are simulated.
32 devices in a mesh: ctx: 8 (over z, y), fsdp: 4 (over x, core).
Axes of the slice: x: 2, y: 2, z: 4, core: 2. Of those that a mesh axis runs over, the one named last changes fastest.
Arguments:
- tokens: bfloat16 [4, 2048, 1024], P('fsdp', 'ctx'), may hold values from -6 to 6
- out_grad: bfloat16 [4, 2048, 1024], P('fsdp', 'ctx'), may hold values from -6 to 6
- lengths: int32 [4, 1], P('fsdp'), may hold values from 512 to 2048, as said below
- norm1_gain: bfloat16 [1024], P('fsdp'), may hold values from 0.5 to 1.5
- w_query: bfloat16 [1024, 1024], P('fsdp'), may hold values from -0.1875 to 0.1875
- w_latent: bfloat16 [1024, 512], P('fsdp'), may hold values from -0.1875 to 0.1875
- w_key_up: bfloat16 [1024, 256], P('fsdp'), may hold values from -0.75 to 0.75
- w_value_up: bfloat16 [1024, 256], P('fsdp'), may hold values from -0.375 to 0.375
- w_output: bfloat16 [1024, 1024], P('fsdp'), may hold values from -1.5 to 1.5
- norm2_gain: bfloat16 [1024], P('fsdp'), may hold values from 0.5 to 1.5
- w_gate: bfloat16 [1024, 2816], P(None, 'fsdp'), may hold values from -0.1875 to 0.1875
- w_up: bfloat16 [1024, 2816], P(None, 'fsdp'), may hold values from -0.1875 to 0.1875
- w_down: bfloat16 [2816, 1024], P('fsdp'), may hold values from -0.109375 to 0.109375
Outputs:
- result: bfloat16 [4, 2048, 1024], P('fsdp', 'ctx')
- token_grad: float32 [4, 2048, 1024], P('fsdp', 'ctx')
- norm1_gain_grad: float32 [1024], P('fsdp')
- w_query_grad: float32 [1024, 1024], P('fsdp')
- w_latent_grad: float32 [1024, 512], P('fsdp')
- w_key_up_grad: float32 [1024, 256], P('fsdp')
- w_value_up_grad: float32 [1024, 256], P('fsdp')
- w_output_grad: float32 [1024, 1024], P('fsdp')
- norm2_gain_grad: float32 [1024], P('fsdp')
- w_gate_grad: float32 [1024, 2816], P(None, 'fsdp')
- w_up_grad: float32 [1024, 2816], P(None, 'fsdp')
- w_down_grad: float32 [2816, 1024], P('fsdp')
Inputs may be any that keep to these rules, and one draw needn't show every extreme that they name: lengths[g, j] valid tokens stand at the start of slot j of group g; the rest of the slot of 2048 rows is padding.
All inputs are finite; a program needn't handle non-finite values.
Results may differ from a plain program's by a relative error of at most 0.025.
Values may be sent and summed in bfloat16 or wider, within the bound.
No kernel may reach another device: no remote copies, remote signals or barrier semaphores. Data moves between devices by JAX's collectives and lax.ppermute only.
A program may use at most 192 MiB of HBM per device.

v0:
```python
import jax
import jax.numpy as jnp
from jax import lax
from jax.sharding import PartitionSpec as P

NH = 16
HD = 64
LAT = 256
GRP = 2
SEQ_MAX = 4096
EPS = 1e-06
NEGATIVE = -1e30


def norm_scale(values):
    return lax.rsqrt(jnp.mean(values * values, axis=-1, keepdims=True) + EPS)


def norm_back(grad_in, normed, scale_rows, gain_full):
    scaled = grad_in * gain_full
    return scale_rows * (scaled - normed * jnp.mean(scaled * normed, axis=-1, keepdims=True))


def key_mask(key_start, key_rows, slot_start, query_pos, length):
    relative = key_start - slot_start + jnp.arange(key_rows, dtype=jnp.int32)
    return (
        (relative[None, :] >= 0)
        & (relative[None, :] <= query_pos[:, None])
        & (relative[None, :] < length)
    )


def raw_scores(query_groups, key_piece, allowed, score_scale):
    grouped = key_piece.reshape(key_piece.shape[0], GRP, LAT)
    scores = (
        jnp.einsum("gpql,kgl->gpqk", query_groups, grouped, preferred_element_type=jnp.float32)
        * score_scale
    )
    return (jnp.where(allowed[None, None], scores, NEGATIVE), grouped)


def on_device(
    tokens,
    out_grad,
    lengths,
    norm1_gain,
    w_query,
    w_latent,
    w_key_up,
    w_value_up,
    w_output,
    norm2_gain,
    w_gate,
    w_up,
    w_down,
):
    ctx_size = lax.axis_size("ctx")
    tok_rows = tokens.shape[1]
    group_rows = tok_rows * ctx_size
    seq_rows = min(SEQ_MAX, group_rows)
    slot_blocks = seq_rows // tok_rows
    head_groups = NH // GRP
    lat_width = GRP * LAT
    my_start = lax.axis_index("ctx") * tok_rows
    slot_number = my_start // seq_rows
    slot_start = slot_number * seq_rows
    length = jnp.sum(
        jnp.where(jnp.arange(lengths.shape[1], dtype=jnp.int32) == slot_number, lengths[0], 0)
    )
    query_pos = my_start - slot_start + jnp.arange(tok_rows, dtype=jnp.int32)
    row_valid = (query_pos < length).astype(jnp.float32)[:, None]
    score_scale = HD ** (-0.5)
    gain_one, query_full, latent_full, key_full, value_full, output_full = (
        lax.all_gather(norm1_gain, "fsdp", axis=0, tiled=True),
        lax.all_gather(w_query, "fsdp", axis=0, tiled=True),
        lax.all_gather(w_latent, "fsdp", axis=0, tiled=True),
        lax.all_gather(w_key_up, "fsdp", axis=0, tiled=True),
        lax.all_gather(w_value_up, "fsdp", axis=0, tiled=True),
        lax.all_gather(w_output, "fsdp", axis=0, tiled=True),
    )
    gain_two, gate_full, up_full, down_full = (
        lax.all_gather(norm2_gain, "fsdp", axis=0, tiled=True),
        lax.all_gather(w_gate, "fsdp", axis=1, tiled=True),
        lax.all_gather(w_up, "fsdp", axis=1, tiled=True),
        lax.all_gather(w_down, "fsdp", axis=0, tiled=True),
    )
    gain_one_f = gain_one.astype(jnp.float32)
    gain_two_f = gain_two.astype(jnp.float32)
    inputs = tokens[0].astype(jnp.float32)
    scale_one = norm_scale(inputs)
    normed_one = inputs * scale_one
    normed = (normed_one * gain_one_f).astype(jnp.bfloat16)
    queries = jnp.dot(normed, query_full, preferred_element_type=jnp.float32).astype(jnp.bfloat16)
    latent = jnp.dot(normed, latent_full, preferred_element_type=jnp.float32).astype(jnp.bfloat16)
    key_heads = key_full.reshape(NH, HD, LAT)
    query_latent = jnp.einsum(
        "shd,hdl->hsl",
        queries.reshape(tok_rows, NH, HD),
        key_heads,
        preferred_element_type=jnp.float32,
    ).astype(jnp.bfloat16)
    query_groups = query_latent.reshape(GRP, head_groups, tok_rows, LAT)

    def is_needed(key_start, key_rows):
        return (
            (key_start + key_rows > slot_start)
            & (key_start < slot_start + length)
            & (key_start < my_start + tok_rows)
        )

    def forward_update(state_now, key_piece, key_start):
        best_now, weight_sum, accum_now = state_now
        allowed = key_mask(key_start, key_piece.shape[0], slot_start, query_pos, length)
        scores, grouped = raw_scores(query_groups, key_piece, allowed, score_scale)
        best_next = jnp.maximum(best_now, jnp.max(scores, axis=-1))
        factor = jnp.exp(best_now - best_next)
        weights = jnp.where(allowed[None, None], jnp.exp(scores - best_next[..., None]), 0.0)
        weight_sum = weight_sum * factor + jnp.sum(weights, axis=-1)
        accum_now = accum_now * factor[..., None] + jnp.einsum(
            "gpqk,kgl->gpql",
            weights.astype(jnp.bfloat16),
            grouped,
            preferred_element_type=jnp.float32,
        )
        return (best_next, weight_sum, accum_now)

    def guarded_forward(state_now, key_piece, key_start):
        return lax.cond(
            is_needed(key_start, key_piece.shape[0]),
            lambda state_in: forward_update(state_in, key_piece, key_start),
            lambda state_in: state_in,
            state_now,
        )

    start_state = (
        jnp.full((GRP, head_groups, tok_rows), NEGATIVE, jnp.float32),
        jnp.zeros((GRP, head_groups, tok_rows), jnp.float32),
        jnp.zeros((GRP, head_groups, tok_rows, LAT), jnp.float32),
    )
    group_latent = lax.all_gather(latent, "ctx", axis=0, tiled=True)

    def forward_loop(block_index, state_now):
        key_start = slot_start + block_index * tok_rows
        key_piece = lax.dynamic_slice_in_dim(group_latent, key_start, tok_rows, 0)
        return guarded_forward(state_now, key_piece, key_start)

    final_state = lax.fori_loop(0, slot_blocks, forward_loop, start_state)
    best_final, sum_final, accum_final = final_state
    log_total = best_final + jnp.log(sum_final)
    mixture = accum_final / sum_final[..., None]
    mixture_low = mixture.astype(jnp.bfloat16)
    value_heads = value_full.reshape(NH, HD, LAT)
    attended = (
        jnp.einsum(
            "hsl,hdl->shd",
            mixture_low.reshape(NH, tok_rows, LAT),
            value_heads,
            preferred_element_type=jnp.float32,
        )
        .reshape(tok_rows, NH * HD)
        .astype(jnp.bfloat16)
    )
    branch = jnp.dot(attended, output_full, preferred_element_type=jnp.float32)
    middle = inputs + branch
    scale_two = norm_scale(middle)
    normed_two_raw = middle * scale_two
    normed_two = (normed_two_raw * gain_two_f).astype(jnp.bfloat16)
    gate_value = jnp.dot(normed_two, gate_full, preferred_element_type=jnp.float32)
    upward = jnp.dot(normed_two, up_full, preferred_element_type=jnp.float32)
    sigmoid_gate = jax.nn.sigmoid(gate_value)
    silu_gate = gate_value * sigmoid_gate
    hidden = (silu_gate * upward).astype(jnp.bfloat16)
    feed_out = jnp.dot(hidden, down_full, preferred_element_type=jnp.float32)
    result = ((middle + feed_out) * row_valid).astype(jnp.bfloat16)
    cotangent = out_grad[0].astype(jnp.float32) * row_valid
    feed_grad = cotangent.astype(jnp.bfloat16)
    down_grad = jnp.einsum("tf,td->fd", hidden, feed_grad, preferred_element_type=jnp.float32)
    hidden_grad = jnp.einsum("td,fd->tf", feed_grad, down_full, preferred_element_type=jnp.float32)
    gate_grad = (
        hidden_grad * upward * sigmoid_gate * (1.0 + gate_value * (1.0 - sigmoid_gate))
    ).astype(jnp.bfloat16)
    up_grad_in = (hidden_grad * silu_gate).astype(jnp.bfloat16)
    gate_w_grad = jnp.einsum("td,tf->df", normed_two, gate_grad, preferred_element_type=jnp.float32)
    up_w_grad = jnp.einsum("td,tf->df", normed_two, up_grad_in, preferred_element_type=jnp.float32)
    normed_two_grad = jnp.einsum(
        "tf,df->td", gate_grad, gate_full, preferred_element_type=jnp.float32
    ) + jnp.einsum("tf,df->td", up_grad_in, up_full, preferred_element_type=jnp.float32)
    gain_two_grad = jnp.sum(normed_two_grad * normed_two_raw, axis=0)
    middle_grad = cotangent + norm_back(normed_two_grad, normed_two_raw, scale_two, gain_two_f)
    branch_grad = middle_grad.astype(jnp.bfloat16)
    output_grad = jnp.einsum("tk,td->kd", attended, branch_grad, preferred_element_type=jnp.float32)
    attended_grad = jnp.einsum(
        "td,kd->tk", branch_grad, output_full, preferred_element_type=jnp.float32
    ).astype(jnp.bfloat16)
    attended_heads = attended_grad.reshape(tok_rows, NH, HD)
    value_grad = jnp.einsum(
        "shd,hsl->hdl",
        attended_heads,
        mixture_low.reshape(NH, tok_rows, LAT),
        preferred_element_type=jnp.float32,
    ).reshape(NH * HD, LAT)
    mixture_grad = (
        jnp.einsum("shd,hdl->hsl", attended_heads, value_heads, preferred_element_type=jnp.float32)
        .astype(jnp.bfloat16)
        .reshape(GRP, head_groups, tok_rows, LAT)
    )
    delta_sum = jnp.sum(mixture_grad * mixture, axis=-1)

    def back_term(query_grad_sum, key_piece, key_start):

        def compute(sum_in):
            allowed = key_mask(key_start, tok_rows, slot_start, query_pos, length)
            scores, grouped = raw_scores(query_groups, key_piece, allowed, score_scale)
            probs = jnp.where(allowed[None, None], jnp.exp(scores - log_total[..., None]), 0.0)
            probs_low = probs.astype(jnp.bfloat16)
            prob_grad = jnp.einsum(
                "gpql,kgl->gpqk", mixture_grad, grouped, preferred_element_type=jnp.float32
            )
            score_grad = (probs * (prob_grad - delta_sum[..., None])).astype(jnp.bfloat16)
            sum_out = sum_in + score_scale * jnp.einsum(
                "gpqk,kgl->gpql", score_grad, grouped, preferred_element_type=jnp.float32
            )
            key_term = score_scale * jnp.einsum(
                "gpqk,gpql->kgl", score_grad, query_groups, preferred_element_type=jnp.float32
            ) + jnp.einsum(
                "gpqk,gpql->kgl", probs_low, mixture_grad, preferred_element_type=jnp.float32
            )
            return (sum_out, key_term.reshape(tok_rows, lat_width))

        def skipped(sum_in):
            return (sum_in, jnp.zeros((tok_rows, lat_width), jnp.float32))

        return lax.cond(is_needed(key_start, tok_rows), compute, skipped, query_grad_sum)

    zero_query = jnp.zeros((GRP, head_groups, tok_rows, LAT), jnp.float32)

    def backward_loop(block_index, state_now):
        sum_now, key_grads = state_now
        key_start = slot_start + block_index * tok_rows
        key_piece = lax.dynamic_slice_in_dim(group_latent, key_start, tok_rows, 0)
        sum_now, key_term = back_term(sum_now, key_piece, key_start)
        key_grads = lax.dynamic_update_slice_in_dim(key_grads, key_term, block_index * tok_rows, 0)
        return (sum_now, key_grads)

    back_start = (zero_query, jnp.zeros((seq_rows, lat_width), jnp.float32))
    query_lat_grad, slot_key_grads = lax.fori_loop(0, slot_blocks, backward_loop, back_start)
    row_count = tok_rows * lax.axis_size("ctx")
    padding = jnp.zeros((row_count, lat_width), jnp.float32)
    padded = jnp.concatenate([padding, slot_key_grads, padding], axis=0)
    offset = jnp.clip(jnp.int32(0) - slot_start + row_count, 0, seq_rows + row_count)
    latent_grad = lax.psum_scatter(
        lax.dynamic_slice_in_dim(padded, offset, row_count, 0).astype(jnp.bfloat16),
        "ctx",
        scatter_dimension=0,
        tiled=True,
    )
    query_lat_low = query_lat_grad.reshape(NH, tok_rows, LAT).astype(jnp.bfloat16)
    key_up_grad = jnp.einsum(
        "shd,hsl->hdl",
        queries.reshape(tok_rows, NH, HD),
        query_lat_low,
        preferred_element_type=jnp.float32,
    ).reshape(NH * HD, LAT)
    query_grad = (
        jnp.einsum("hsl,hdl->shd", query_lat_low, key_heads, preferred_element_type=jnp.float32)
        .reshape(tok_rows, NH * HD)
        .astype(jnp.bfloat16)
    )
    query_w_grad = jnp.einsum("td,tk->dk", normed, query_grad, preferred_element_type=jnp.float32)
    latent_w_grad = jnp.einsum("td,tk->dk", normed, latent_grad, preferred_element_type=jnp.float32)
    normed_grad = jnp.einsum(
        "tk,dk->td", query_grad, query_full, preferred_element_type=jnp.float32
    ) + jnp.einsum("tk,dk->td", latent_grad, latent_full, preferred_element_type=jnp.float32)
    gain_one_grad = jnp.sum(normed_grad * normed_one, axis=0)
    input_grad = middle_grad + norm_back(normed_grad, normed_one, scale_one, gain_one_f)
    shards = (
        lax.psum_scatter(
            gain_one_grad.astype(jnp.bfloat16), "fsdp", scatter_dimension=0, tiled=True
        ).astype(jnp.float32),
        lax.psum_scatter(
            query_w_grad.astype(jnp.bfloat16), "fsdp", scatter_dimension=0, tiled=True
        ).astype(jnp.float32),
        lax.psum_scatter(
            latent_w_grad.astype(jnp.bfloat16), "fsdp", scatter_dimension=0, tiled=True
        ).astype(jnp.float32),
        lax.psum_scatter(
            key_up_grad.astype(jnp.bfloat16), "fsdp", scatter_dimension=0, tiled=True
        ).astype(jnp.float32),
        lax.psum_scatter(
            value_grad.astype(jnp.bfloat16), "fsdp", scatter_dimension=0, tiled=True
        ).astype(jnp.float32),
        lax.psum_scatter(
            output_grad.astype(jnp.bfloat16), "fsdp", scatter_dimension=0, tiled=True
        ).astype(jnp.float32),
        lax.psum_scatter(
            gain_two_grad.astype(jnp.bfloat16), "fsdp", scatter_dimension=0, tiled=True
        ).astype(jnp.float32),
        lax.psum_scatter(
            gate_w_grad.astype(jnp.bfloat16), "fsdp", scatter_dimension=1, tiled=True
        ).astype(jnp.float32),
        lax.psum_scatter(
            up_w_grad.astype(jnp.bfloat16), "fsdp", scatter_dimension=1, tiled=True
        ).astype(jnp.float32),
        lax.psum_scatter(
            down_grad.astype(jnp.bfloat16), "fsdp", scatter_dimension=0, tiled=True
        ).astype(jnp.float32),
    )
    summed = (
        lax.psum(shards[0].astype(jnp.bfloat16), "ctx").astype(jnp.float32),
        lax.psum(shards[1].astype(jnp.bfloat16), "ctx").astype(jnp.float32),
        lax.psum(shards[2].astype(jnp.bfloat16), "ctx").astype(jnp.float32),
        lax.psum(shards[3].astype(jnp.bfloat16), "ctx").astype(jnp.float32),
        lax.psum(shards[4].astype(jnp.bfloat16), "ctx").astype(jnp.float32),
        lax.psum(shards[5].astype(jnp.bfloat16), "ctx").astype(jnp.float32),
        lax.psum(shards[6].astype(jnp.bfloat16), "ctx").astype(jnp.float32),
        lax.psum(shards[7].astype(jnp.bfloat16), "ctx").astype(jnp.float32),
        lax.psum(shards[8].astype(jnp.bfloat16), "ctx").astype(jnp.float32),
        lax.psum(shards[9].astype(jnp.bfloat16), "ctx").astype(jnp.float32),
    )
    return (
        result[None],
        input_grad[None],
        summed[0],
        summed[1],
        summed[2],
        summed[3],
        summed[4],
        summed[5],
        summed[6],
        summed[7],
        summed[8],
        summed[9],
    )


def solution(mesh):
    return jax.shard_map(
        on_device,
        mesh=mesh,
        in_specs=(
            P("fsdp", "ctx", None),
            P("fsdp", "ctx", None),
            P("fsdp", None),
            P("fsdp"),
            P("fsdp", None),
            P("fsdp", None),
            P("fsdp", None),
            P("fsdp", None),
            P("fsdp", None),
            P("fsdp"),
            P(None, "fsdp"),
            P(None, "fsdp"),
            P("fsdp", None),
        ),
        out_specs=(
            P("fsdp", "ctx", None),
            P("fsdp", "ctx", None),
            P("fsdp"),
            P("fsdp", None),
            P("fsdp", None),
            P("fsdp", None),
            P("fsdp", None),
            P("fsdp", None),
            P("fsdp"),
            P(None, "fsdp"),
            P(None, "fsdp"),
            P("fsdp", None),
        ),
        check_vma=False,
    )
```

profile of v0, /device:TPU:0, one launch (start us, length us, event | category | flops | bytes accessed | tf_op | source)
XLA Modules:
  0.0 1036.9 jit_solution(728526672755502800)
XLA Ops:
  9.4 6.0 all-gather
  16.6 12.5 %all-gather.10.cloned.1.call-done = bf16[1024,512]{1,0:T(8,128)(2,1)} async-done(((bf16[256,512]{1,0:T(8,128)(2,1)}), bf16[1024,512]{1,0:T(8,128)(2,1)}) %all-gather.10.cloned.1.call-update) | async-done | bytes 1048592 | tf_op jit(solution)/shard_map/all_gather | solution.py:76
  29.0 2.6 convolution_convert_fusion.14
  34.9 5.1 all-gather.1
  40.0 10.9 %all_gather.38 = bf16[1024,256]{1,0:T(8,128)(2,1)} all-gather(bf16[256,256]{1,0:T(8,128)(2,1)S(1)} %copy-done.41), channel_id=1, replica_groups=mesh['ctx'=8,'fsdp'=4] {'fsdp'}, dimensions={0}, use_global_device_ids=true | all-gather | bytes 655360 | tf_op jit(solution)/shard_map/all_gather | solution.py:78
  50.9 7.3 all_gather.37
  58.2 2.5 convolution_convert_fusion.13
  63.0 2.9 copy.75
  65.9 42.2 %all-gather.12.cloned.1.call-done = bf16[2048,512]{1,0:T(8,128)(2,1)} async-done(((bf16[256,512]{1,0:T(8,128)(2,1)}), bf16[2048,512]{1,0:T(8,128)(2,1)}) %all-gather.12.cloned.1.call-update) | async-done | bytes 2097168 | tf_op jit(solution)/shard_map/all_gather | solution.py:140
  108.1 3.9 copy.70
  114.5 10.8 %while.41 = (s32[]{:T(128)}, f32[2,8,256]{2,1,0:T(8,128)S(1)}, f32[2,8,256]{2,1,0:T(8,128)S(1)}, f32[2,8,256,256]{3,2,1,0:T(8,128)}, s32[]{:T(128)}, /*index=5*/...) while((s32[]{:T(128)}, f32[2,8,256]{2,1,0:T(8,128)S(1)}, ...), condition=%wide.region_6.7_spmd.clone, body=%wide.region_1.6_spmd.clone.sunk | while | flops 1089676544 | bytes 58203600 | solution.py:147
  114.5 10.4 %conditional.6 = ((f32[2,8,256]{2,1,0:T(8,128)S(1)}, f32[2,8,256]{2,1,0:T(8,128)S(1)}, f32[2,8,256,256]{3,2,1,0:T(8,128)})) conditional(s32[]{:T(128)} %convert_element_type.380, (f32[2,8,256]{2,1,0:T(8,128)S(1)}, f32[2,8,256]{2,1,0:T(8,128)S(1)}, f32[2,8,256,256]{3,2,1,0:T(8,128)}) %tuple.129, (s32[]{:T(128)}, s32[]{:T(128)}, s32[]{:T(128)}, ...), branch_computations={%region_2.2_spmd, %region_3.5_spmd} | conditional | flops 1089676544 | bytes 58202268 | solution.py:128
  115.8 2.8 fusion.4
  125.2 5.9 copy.71
  131.1 2.7 fusion.44
  135.6 2.6 multiply_reduce_fusion.3
  139.3 36.1 %all-gather.18.cloned.1.call-done = bf16[1024,2816]{0,1:T(8,128)(2,1)} async-done(((bf16[1024,704]{0,1:T(8,128)(2,1)}), bf16[1024,2816]{0,1:T(8,128)(2,1)}) %all-gather.18.cloned.1.call-update) | async-done | bytes 5767184 | tf_op jit(solution)/shard_map/all_gather | solution.py:83
  175.4 5.9 fusion.79
  181.4 38.9 %all-gather.20.cloned.1.call-done = bf16[1024,2816]{0,1:T(8,128)(2,1)} async-done(((bf16[1024,704]{0,1:T(8,128)(2,1)}), bf16[1024,2816]{0,1:T(8,128)(2,1)}) %all-gather.20.cloned.1.call-update) | async-done | bytes 5767184 | tf_op jit(solution)/shard_map/all_gather | solution.py:84
  220.3 5.9 fusion.80
  226.2 39.1 %all-gather.22.cloned.1.call-done = bf16[2816,1024]{1,0:T(8,128)(2,1)} async-done(((bf16[704,1024]{1,0:T(8,128)(2,1)}), bf16[2816,1024]{1,0:T(8,128)(2,1)}) %all-gather.22.cloned.1.call-update) | async-done | bytes 5767184 | tf_op jit(solution)/shard_map/all_gather | solution.py:85
  265.3 8.2 multiply_convert_fusion
  273.5 5.4 fusion.81
  288.6 3.7 multiply_reduce_fusion
  296.3 20.4 %while.42 = (s32[]{:T(128)}, f32[2,8,256,256]{3,2,1,0:T(8,128)}, bf16[2048,512]{0,1:T(8,128)(2,1)}, s32[]{:T(128)}, s32[]{:T(128)}, /*index=5*/s32[]{:T(128)}, s...) while((s32[]{:T(128)}, f32[2,8,256,256]{3,2,1,0:T(8,128)}, ...), condition=%wide.region_13.14_spmd.clone, body=%wide.region_10.13_spmd.clone.sunk | while | flops 2699625728 | bytes 97771040 | solution.py:246
  296.3 14.2 %conditional.7 = (f32[2,8,256,256]{3,2,1,0:T(8,128)}, bf16[256,512]{0,1:T(8,128)(2,1)S(1)}) conditional(s32[]{:T(128)} %convert_element_type.381, f32[2,8,256,256]{3,2,1,0:T(8,128)} %get-tuple-element.1157, (s32[]{:T(128)}, s32[]{:T(128)}, s32[]{:T(128)}, s32[]{:T(128)}, bf16[2048,512]{0,1:T(8,128)(2,1)}, ...), branch_computations={%region_11.11_spmd, %region_12.12_spmd} | conditional | flops 2699625728 | bytes 97245368 | solution.py:233
  297.5 2.8 fusion.78
  300.4 4.5 fusion.18
  318.3 4.3 fusion.42
  322.7 2.5 convert_element_type.249
  327.9 2.7 convolution_convert_fusion.9
  337.6 152.6 %reduce-scatter.10.cloned.1.call-done = bf16[256,512]{0,1:T(8,128)(2,1)} async-done(((bf16[2048,512]{0,1:T(8,128)(2,1)}), bf16[256,512]{0,1:T(8,128)(2,1)}) %reduce-scatter.10.cloned.1.call-update) | async-done | bytes 262160 | tf_op jit(solution)/shard_map/reduce_scatter | solution.py:251
  490.3 2.5 convolution_convert_fusion.7
  492.8 5.5 convolution_convert_fusion.2
  498.4 5.7 convolution_convert_fusion.1
  505.5 5.3 convolution_convert_fusion
  510.8 2.6 reduce-scatter.16.cloned.1.call-done
  513.4 24.2 %reduce-scatter.18.cloned.1.call-done = bf16[256,256]{1,0:T(8,128)(2,1)} async-done(((bf16[1024,256]{1,0:T(8,128)(2,1)}), bf16[256,256]{1,0:T(8,128)(2,1)}) %reduce-scatter.18.cloned.1.call-update) | async-done | bytes 131088 | tf_op jit(solution)/shard_map/reduce_scatter | solution.py:289
  537.6 34.6 %reduce-scatter.12.cloned.1.call-done = bf16[256,1024]{1,0:T(8,128)(2,1)} async-done(((bf16[1024,1024]{1,0:T(8,128)(2,1)}), bf16[256,1024]{1,0:T(8,128)(2,1)}) %reduce-scatter.12.cloned.1.call-update) | async-done | bytes 524304 | tf_op jit(solution)/shard_map/reduce_scatter | solution.py:280
  572.2 34.6 %reduce-scatter.20.cloned.1.call-done = bf16[256,1024]{1,0:T(8,128)(2,1)} async-done(((bf16[1024,1024]{1,0:T(8,128)(2,1)}), bf16[256,1024]{1,0:T(8,128)(2,1)}) %reduce-scatter.20.cloned.1.call-update) | async-done | bytes 524304 | tf_op jit(solution)/shard_map/reduce_scatter | solution.py:292
  606.8 28.0 %reduce-scatter.14.cloned.1.call-done = bf16[256,512]{1,0:T(8,128)(2,1)} async-done(((bf16[1024,512]{1,0:T(8,128)(2,1)}), bf16[256,512]{1,0:T(8,128)(2,1)}) %reduce-scatter.14.cloned.1.call-update) | async-done | bytes 262160 | tf_op jit(solution)/shard_map/reduce_scatter | solution.py:283
  634.8 57.5 %reduce-scatter.22.cloned.1.call-done = bf16[1024,704]{0,1:T(8,128)(2,1)} async-done(((bf16[1024,2816]{0,1:T(8,128)(2,1)}), bf16[1024,704]{0,1:T(8,128)(2,1)}) %reduce-scatter.22.cloned.1.call-update) | async-done | bytes 1441808 | tf_op jit(solution)/shard_map/reduce_scatter | solution.py:298
  692.3 57.3 %reduce-scatter.24.cloned.1.call-done = bf16[1024,704]{0,1:T(8,128)(2,1)} async-done(((bf16[1024,2816]{0,1:T(8,128)(2,1)}), bf16[1024,704]{0,1:T(8,128)(2,1)}) %reduce-scatter.24.cloned.1.call-update) | async-done | bytes 1441808 | tf_op jit(solution)/shard_map/reduce_scatter | solution.py:301
  749.6 57.5 %reduce-scatter.26.cloned.1.call-done = bf16[704,1024]{1,0:T(8,128)(2,1)} async-done(((bf16[2816,1024]{1,0:T(8,128)(2,1)}), bf16[704,1024]{1,0:T(8,128)(2,1)}) %reduce-scatter.26.cloned.1.call-update) | async-done | bytes 1441808 | tf_op jit(solution)/shard_map/reduce_scatter | solution.py:304
  811.4 5.3 fusion.53
  817.5 6.1 all-reduce.4
  823.7 22.1 %all-reduce.2 = (bf16[256]{0:T(256)(128)(2,1)S(1)}, bf16[256]{0:T(256)(128)(2,1)S(1)}) all-reduce(bf16[256]{0:T(256)(128)(2,1)S(1)} %dynamic-slice.1, bf16[256]{0:T(256)(128)(2,1)S(1)} %dynamic-slice.3), channel_id=1, replica_groups=mesh['ctx'=8,'fsdp'=4] {'ctx'}, use_global_device_ids=true, to_apply=%region_18.19 | all-reduce | flops 512 | bytes 2048 | tf_op jit(solution)/shard_map/psum | solution.py:309
  848.2 167.7 %all-reduce.7.cloned.1.call-done = (bf16[256,1024]{1,0:T(8,128)(2,1)}, bf16[256,512]{1,0:T(8,128)(2,1)}, bf16[256,256]{1,0:T(8,128)(2,1)}, bf16[256,256]{1,0:T(8...) async-done(((bf16[256,1024]{1,0:T(8,128)(2,1)}, bf16[256,512]{1,0:T(8,128)(2,1)}, ...) | async-done | bytes 5898256 | tf_op jit(solution)/shard_map/psum | solution.py:310
  (235 shorter events, 81.9 us)
Async XLA Ops:
  7.2 21.8 %all-gather.10.cloned.1.call-start = ((), (), s32[]{:S(2)}) async-start(), calls=%async_computation.9 | async-start | bytes 1310720 | tf_op jit(solution)/shard_map/all_gather | solution.py:76
  7.9 50.3 %all-gather.14.cloned.1.call-start = ((), (), s32[]{:S(2)}) async-start(), calls=%async_computation.11 | async-start | bytes 2621440 | tf_op jit(solution)/shard_map/all_gather | solution.py:75
  8.7 99.4 %all-gather.12.cloned.1.call-start = ((), (), s32[]{:S(2)}) async-start(), calls=%async_computation.10 | async-start | bytes 2359296 | tf_op jit(solution)/shard_map/all_gather | solution.py:140
  31.6 3.3 copy-start.44
  31.6 8.4 copy-start.41
  31.6 19.3 %copy-start.42 = (bf16[256,256]{1,0:T(8,128)(2,1)S(1)}, bf16[256,256]{1,0:T(8,128)(2,1)}, u32[]{:S(2)}) copy-start(bf16[256,256]{1,0:T(8,128)(2,1)} %param.27) | copy-start | bytes 393220
  31.6 104.0 %all-gather.16.cloned.1.call-start = ((), (), s32[]{:S(2)}) async-start(), calls=%async_computation.12 | async-start | bytes 2621440 | tf_op jit(solution)/shard_map/all_gather | solution.py:79
  32.2 26.0 %copy-start.8 = (bf16[1,256,1024]{2,1,0:T(8,128)(2,1)S(1)}, bf16[1,256,1024]{2,1,0:T(8,128)(2,1)}, u32[]{:S(2)}) copy-start(bf16[1,256,1024]{2,1,0:T(8,128)(2,1)} %param.21) | copy-start | bytes 1572868
  32.2 143.2 %all-gather.18.cloned.1.call-start = ((), (), s32[]{:S(2)}) async-start(), calls=%async_computation.13 | async-start | bytes 7208960 | tf_op jit(solution)/shard_map/all_gather | solution.py:83
  32.8 187.5 %all-gather.20.cloned.1.call-start = ((), (), s32[]{:S(2)}) async-start(), calls=%async_computation.14 | async-start | bytes 7208960 | tf_op jit(solution)/shard_map/all_gather | solution.py:84
  33.4 231.9 %all-gather.22.cloned.1.call-start = ((), (), s32[]{:S(2)}) async-start(), calls=%async_computation.15 | async-start | bytes 7208960 | tf_op jit(solution)/shard_map/all_gather | solution.py:85
  34.1 456.1 %reduce-scatter.10.cloned.1.call-start = ((), (), s32[]{:S(2)}) async-start(), calls=%async_computation.16 | async-start | bytes 2359296 | tf_op jit(solution)/shard_map/reduce_scatter | solution.py:251
  58.2 4.8 copy-start.22
  118.6 2.2 copy-start
  131.1 4.0 copy-start.24
  135.6 2.7 copy-start.20
  139.3 81.0 %copy-start.18 = (bf16[256,1024]{1,0:T(8,128)(2,1)}, bf16[256,1024]{1,0:T(8,128)(2,1)S(1)}, u32[]{:S(2)}) copy-start(bf16[256,1024]{1,0:T(8,128)(2,1)S(1)} %multiply_convert_fusion.3) | copy-start | bytes 1572868
  273.5 5.4 copy-start.34
  273.5 5.4 copy-start.33
  273.5 5.4 copy-start.12
  273.5 5.7 copy-start.43
  283.2 3.6 copy-start.25
  288.6 3.8 copy-start.15
  300.4 4.5 copy-start.2
  305.0 2.9 copy-start.16
  322.6 190.8 %reduce-scatter.16.cloned.1.call-start = ((), (), s32[]{:S(2)}) async-start(), calls=%async_computation.19 | async-start | bytes 655360 | tf_op jit(solution)/shard_map/reduce_scatter | solution.py:286
  322.7 3.8 copy-start.29
  325.2 2.7 copy-start.6
  327.8 2.8 copy-start.23
  327.8 209.8 %reduce-scatter.18.cloned.1.call-start = ((), (), s32[]{:S(2)}) async-start(), calls=%async_computation.20 | async-start | bytes 655360 | tf_op jit(solution)/shard_map/reduce_scatter | solution.py:289
  330.6 241.6 %reduce-scatter.12.cloned.1.call-start = ((), (), s32[]{:S(2)}) async-start(), calls=%async_computation.17 | async-start | bytes 2621440 | tf_op jit(solution)/shard_map/reduce_scatter | solution.py:280
  333.0 4.5 copy-start.26
  333.0 2.5 copy-start.10
  333.0 2.5 copy-start.21
  335.2 271.6 %reduce-scatter.20.cloned.1.call-start = ((), (), s32[]{:S(2)}) async-start(), calls=%async_computation.21 | async-start | bytes 2621440 | tf_op jit(solution)/shard_map/reduce_scatter | solution.py:292
  337.5 155.3 %copy-start.19 = (bf16[256,1024]{1,0:T(8,128)(2,1)S(1)}, bf16[256,1024]{1,0:T(8,128)(2,1)}, u32[]{:S(2)}) copy-start(bf16[256,1024]{1,0:T(8,128)(2,1)} %copy-done.18) | copy-start | bytes 1572868
  337.6 297.3 %reduce-scatter.14.cloned.1.call-start = ((), (), s32[]{:S(2)}) async-start(), calls=%async_computation.18 | async-start | bytes 1310720 | tf_op jit(solution)/shard_map/reduce_scatter | solution.py:283
  492.8 199.5 %reduce-scatter.22.cloned.1.call-start = ((), (), s32[]{:S(2)}) async-start(), calls=%async_computation.22 | async-start | bytes 7208960 | tf_op jit(solution)/shard_map/reduce_scatter | solution.py:298
  498.4 251.2 %reduce-scatter.24.cloned.1.call-start = ((), (), s32[]{:S(2)}) async-start(), calls=%async_computation.23 | async-start | bytes 7208960 | tf_op jit(solution)/shard_map/reduce_scatter | solution.py:301
  504.1 302.9 %reduce-scatter.26.cloned.1.call-start = ((), (), s32[]{:S(2)}) async-start(), calls=%async_computation.24 | async-start | bytes 7208960 | tf_op jit(solution)/shard_map/reduce_scatter | solution.py:304
  510.8 505.1 %all-reduce.7.cloned.1.call-start = ((), (), s32[]{:S(2)}) async-start(), calls=%async_computation.25 | async-start | bytes 11796480 | tf_op jit(solution)/shard_map/psum | solution.py:310
  807.1 4.3 copy-start.13
  808.9 2.5 copy-start.31
  811.4 5.3 copy-start.38
  811.4 5.3 copy-start.39
  1015.9 7.3 copy-start.40
  1015.9 8.4 copy-start.37
  1023.2 3.0 copy-start.36
  (15 other events, 24.3 us)
Sparse Core Ops, SparseCore 0:
  9.6 19.4 all-gather.9
  30.6 25.3 all-gather.13
  58.7 49.3 all-gather.11
  109.5 21.0 all-gather.15
  132.0 43.3 all-gather.17
  176.9 43.3 all-gather.19
  221.9 43.3 all-gather.21
  322.7 167.4 reduce-scatter.9
  492.7 20.6 reduce-scatter.15
  515.9 21.6 reduce-scatter.17
  540.7 31.4 reduce-scatter.11
  575.3 31.4 reduce-scatter.19
  609.9 24.8 reduce-scatter.13
  637.4 54.8 reduce-scatter.21
  694.7 54.8 reduce-scatter.23
  752.1 54.8 reduce-scatter.25
  811.5 204.3 all-reduce.6
where the time goes:
time: 1050 us; the launch traced here: 1040 us
  waiting for transfers between devices  789 us (75%)
  matrix products  94.2 us (9%)
  blocking collectives  57.4 us (5%)
  local copies, waits for them, and re-layouts  45.5 us (4%)
  other arithmetic  33 us (3%)
  between operations  16 us (2%)
    psum x1, waiting for transfers between devices, on_device(): lax.psum(shards[1].astype(jnp.bfloat16), 'ctx').astype(jnp.float32)  168 us
    reduce_scatter x1, waiting for transfers between devices, on_device(): lax.psum_scatter(lax.dynamic_slice_in_dim(padded, offset, row_count, 0).a...  153 us
    reduce_scatter x1, waiting for transfers between devices, on_device(): lax.psum_scatter(gate_w_grad.astype(jnp.bfloat16), 'fsdp', scatter_dimens...  57.5 us
    reduce_scatter x1, waiting for transfers between devices, on_device(): lax.psum_scatter(down_grad.astype(jnp.bfloat16), 'fsdp', scatter_dimensio...  57.5 us
    reduce_scatter x1, waiting for transfers between devices, on_device(): lax.psum_scatter(up_w_grad.astype(jnp.bfloat16), 'fsdp', scatter_dimensio...  57.3 us
    all_gather x1, waiting for transfers between devices, on_device(): group_latent = lax.all_gather(latent, 'ctx', axis=0, tiled=True)  42.2 us
    all_gather x1, waiting for transfers between devices, on_device(): lax.all_gather(w_down, 'fsdp', axis=0, tiled=True)  39.1 us
    all_gather x1, waiting for transfers between devices, on_device(): lax.all_gather(w_up, 'fsdp', axis=1, tiled=True)  38.9 us
  transfers between devices with their start and end apart: 17, of which 15 were waited for; matrix products, arithmetic and copies ran while one was open for 9% of the time, Pallas kernels for 0%

commit v1 on v0

--- a/solution.py
+++ b/solution.py
@@ -78,11 +78,28 @@
         lax.all_gather(w_value_up, "fsdp", axis=0, tiled=True),
         lax.all_gather(w_output, "fsdp", axis=0, tiled=True),
     )
+
+    def state_samples(x_local, chip_axis):
+        y_new = lax.axis_index(chip_axis)
+        back = lax.axis_size(chip_axis)
+        arr_next, top, big = (back, y_new, x_local.shape[0])
+        crops = []
+        for c in tuple(range(arr_next)):
+            crops.append((c, (c + 1) % arr_next))
+        lower = x_local
+        w1 = jnp.zeros((*x_local.shape[:0], arr_next * big, *x_local.shape[1:]), x_local.dtype)
+        for num in [*range(arr_next)]:
+            newest = (top - num) % arr_next
+            w1 = lax.dynamic_update_slice_in_dim(w1, lower, newest * big, axis=0)
+            if num < arr_next - 1:
+                lower = lax.ppermute(lower, chip_axis, perm=crops)
+        return w1
+
     gain_two, gate_full, up_full, down_full = (
         lax.all_gather(norm2_gain, "fsdp", axis=0, tiled=True),
         lax.all_gather(w_gate, "fsdp", axis=1, tiled=True),
         lax.all_gather(w_up, "fsdp", axis=1, tiled=True),
-        lax.all_gather(w_down, "fsdp", axis=0, tiled=True),
+        state_samples(w_down, "fsdp"),
     )
     gain_one_f = gain_one.astype(jnp.float32)
     gain_two_f = gain_two.astype(jnp.float32)

time: 1050 us -> 992 us (0.945)
  waiting for transfers between devices: 789 us -> 716 us
  blocking collectives: 57.4 us -> 77.9 us
  local copies, waits for them, and re-layouts: 45.5 us -> 61.1 us
  matrix products: 94.2 us -> 81.9 us
    all_gather x1, waiting for transfers between devices: 42.2 us -> 0.01 us  [on_device(): group_latent = lax.all_gather(latent, 'ctx', axis=0, tiled=True)]
    all_gather x1 -> x0, waiting for transfers between devices: 39.1 us -> none  [on_device(): lax.all_gather(w_down, 'fsdp', axis=0, tiled=True)]
    ppermute x0 -> x3, waiting for transfers between devices: none -> 29.4 us  [state_samples(): lower = lax.ppermute(lower, chip_axis, perm=crops)]
    reduce_scatter x1, waiting for transfers between devices: 2.6 us -> 24.9 us  [on_device(): lax.psum_scatter(key_up_grad.astype(jnp.bfloat16), 'fsdp', scatter_dimens...]
    reduce_scatter x1, waiting for transfers between devices: 24.2 us -> 4.89 us  [on_device(): lax.psum_scatter(value_grad.astype(jnp.bfloat16), 'fsdp', scatter_dimensi...]
    all_gather x1, waiting for transfers between devices: 36.1 us -> 18.2 us  [on_device(): lax.all_gather(w_gate, 'fsdp', axis=1, tiled=True)]
    all_gather x1, blocking collectives: 5.07 us -> 18.6 us  [on_device(): lax.all_gather(norm2_gain, 'fsdp', axis=0, tiled=True)]
  transfers between devices with their start and end apart: 17 -> 19, of which waited for: 15 -> 14; matrix products, arithmetic and copies ran while one was open for 9% -> 10% of each run, Pallas kernels for 0% -> 0%
where the time goes in v1:
time: 992 us; the launch traced here: 986 us
  waiting for transfers between devices  716 us (72%)
  matrix products  81.9 us (8%)
  blocking collectives  77.9 us (8%)
  local copies, waits for them, and re-layouts  61.1 us (6%)
  other arithmetic  30.4 us (3%)
  between operations  16.1 us (2%)
    psum x1, waiting for transfers between devices, on_device(): lax.psum(shards[1].astype(jnp.bfloat16), 'ctx').astype(jnp.float32)  168 us
    reduce_scatter x1, waiting for transfers between devices, on_device(): lax.psum_scatter(lax.dynamic_slice_in_dim(padded, offset, row_count, 0).a...  147 us
    reduce_scatter x1, waiting for transfers between devices, on_device(): lax.psum_scatter(gate_w_grad.astype(jnp.bfloat16), 'fsdp', scatter_dimens...  57.6 us
    reduce_scatter x1, waiting for transfers between devices, on_device(): lax.psum_scatter(down_grad.astype(jnp.bfloat16), 'fsdp', scatter_dimensio...  57.5 us
    reduce_scatter x1, waiting for transfers between devices, on_device(): lax.psum_scatter(up_w_grad.astype(jnp.bfloat16), 'fsdp', scatter_dimensio...  57.3 us
    all_gather x1, waiting for transfers between devices, on_device(): lax.all_gather(w_up, 'fsdp', axis=1, tiled=True)  38.9 us
    reduce_scatter x1, waiting for transfers between devices, on_device(): lax.psum_scatter(query_w_grad.astype(jnp.bfloat16), 'fsdp', scatter_dimen...  34.7 us
    reduce_scatter x1, waiting for transfers between devices, on_device(): lax.psum_scatter(output_grad.astype(jnp.bfloat16), 'fsdp', scatter_dimens...  34.4 us
  transfers between devices with their start and end apart: 19, of which 14 were waited for; matrix products, arithmetic and copies ran while one was open for 10% of the time, Pallas kernels for 0%

profile of v1, /device:TPU:0, one launch (start us, length us, event | category | flops | bytes accessed | tf_op | source)
XLA Modules:
  0.0 985.7 jit_solution(1505287876093324529)
XLA Ops:
  9.4 6.0 all-gather
  16.6 12.4 %all-gather.9.cloned.1.call-done = bf16[1024,512]{1,0:T(8,128)(2,1)} async-done(((bf16[256,512]{1,0:T(8,128)(2,1)}), bf16[1024,512]{1,0:T(8,128)(2,1)}) %all-gather.9.cloned.1.call-update) | async-done | bytes 1048592 | tf_op jit(solution)/shard_map/all_gather | solution.py:76
  29.0 2.7 convolution_convert_fusion.14
  33.8 29.4 %collective-permute-done = bf16[704,1024]{1,0:T(8,128)(2,1)S(1)} collective-permute-done((bf16[704,1024]{1,0:T(8,128)(2,1)S(1)}, bf16[704,1024]{1,0:T(8,128)(2,1)S(1)}, u32[]{:S(2)}, u32[]{:S(2)}) %collective-permute-start) | collective-permute-done | bytes 1441824 | tf_op jit(solution)/shard_map/ppermute | solution.py:95
  64.0 18.6 %all-gather.1 = bf16[4,1,256]{2,1,0:T(2,128)(2,1)S(1)} all-gather(bf16[1,1,256]{2,1,0:T(2,128)(2,1)S(1)} %reshape.281), channel_id=1, replica_groups=mesh['ctx'=8,'fsdp'=4] {'fsdp'}, dimensions={0}, use_global_device_ids=true | all-gather | bytes 2560 | tf_op jit(solution)/shard_map/all_gather | solution.py:99
  82.8 3.2 broadcast_in_dim.88
  87.3 17.7 %all_gather.34 = bf16[1024,256]{1,0:T(8,128)(2,1)S(1)} all-gather(bf16[256,256]{1,0:T(8,128)(2,1)S(1)} %copy-done.39), channel_id=1, replica_groups=mesh['ctx'=8,'fsdp'=4] {'fsdp'}, dimensions={0}, use_global_device_ids=true | all-gather | bytes 655360 | tf_op jit(solution)/shard_map/all_gather | solution.py:77
  104.9 7.5 all_gather.35
  112.5 2.7 constant_dynamic-update-slice_fusion.3
  115.1 2.6 constant_dynamic-update-slice_fusion.2
  117.8 2.7 convolution_convert_fusion.13
  122.8 3.4 copy.75
  126.1 2.6 constant_dynamic-update-slice_fusion.1
  128.7 3.9 copy.70
  135.2 11.2 %while.41 = (s32[]{:T(128)}, f32[2,8,256]{2,1,0:T(8,128)S(1)}, f32[2,8,256]{2,1,0:T(8,128)S(1)}, f32[2,8,256,256]{3,2,1,0:T(8,128)}, s32[]{:T(128)}, /*index=5*/...) while((s32[]{:T(128)}, f32[2,8,256]{2,1,0:T(8,128)S(1)}, ...), condition=%wide.region_6.7_spmd.clone, body=%wide.region_1.0_spmd.clone.sunk | while | flops 1089676544 | bytes 58203592 | solution.py:164
  135.2 10.8 %conditional.6 = ((f32[2,8,256]{2,1,0:T(8,128)S(1)}, f32[2,8,256]{2,1,0:T(8,128)S(1)}, f32[2,8,256,256]{3,2,1,0:T(8,128)})) conditional(s32[]{:T(128)} %convert_element_type.380, (f32[2,8,256]{2,1,0:T(8,128)S(1)}, f32[2,8,256]{2,1,0:T(8,128)S(1)}, f32[2,8,256,256]{3,2,1,0:T(8,128)}) %tuple.129, (s32[]{:T(128)}, s32[]{:T(128)}, s32[]{:T(128)}, ...), branch_computations={%region_2.2_spmd, %region_3.5_spmd} | conditional | flops 1089676544 | bytes 58202268 | solution.py:145
  136.6 2.7 fusion.4
  146.4 5.4 copy.71
  151.8 2.7 fusion.44
  156.4 2.6 multiply_reduce_fusion.3
  160.1 18.2 %all-gather.17.cloned.1.call-done = bf16[1024,2816]{0,1:T(8,128)(2,1)} async-done(((bf16[1024,704]{0,1:T(8,128)(2,1)}), bf16[1024,2816]{0,1:T(8,128)(2,1)}) %all-gather.17.cloned.1.call-update) | async-done | bytes 5767184 | tf_op jit(solution)/shard_map/all_gather | solution.py:100
  178.3 5.9 fusion.79
  184.2 38.9 %all-gather.19.cloned.1.call-done = bf16[1024,2816]{0,1:T(8,128)(2,1)} async-done(((bf16[1024,704]{0,1:T(8,128)(2,1)}), bf16[1024,2816]{0,1:T(8,128)(2,1)}) %all-gather.19.cloned.1.call-update) | async-done | bytes 5767184 | tf_op jit(solution)/shard_map/all_gather | solution.py:101
  223.1 4.5 fusion.80
  227.7 8.8 multiply_convert_fusion
  247.9 3.6 multiply_reduce_fusion
  255.5 17.4 %while.42 = (s32[]{:T(128)}, f32[2,8,256,256]{3,2,1,0:T(8,128)}, bf16[2048,512]{0,1:T(8,128)(2,1)}, s32[]{:T(128)}, s32[]{:T(128)}, /*index=5*/s32[]{:T(128)}, s...) while((s32[]{:T(128)}, f32[2,8,256,256]{3,2,1,0:T(8,128)}, ...), condition=%wide.region_13.14_spmd.clone, body=%wide.region_10.13_spmd.clone.sunk | while | flops 2699625728 | bytes 80993792 | solution.py:263
  255.5 11.1 %conditional.7 = (f32[2,8,256,256]{3,2,1,0:T(8,128)}, bf16[256,512]{0,1:T(8,128)(2,1)S(1)}) conditional(s32[]{:T(128)} %convert_element_type.381, f32[2,8,256,256]{3,2,1,0:T(8,128)} %get-tuple-element.1157, (s32[]{:T(128)}, s32[]{:T(128)}, s32[]{:T(128)}, s32[]{:T(128)}, bf16[2048,512]{0,1:T(8,128)(2,1)}, ...), branch_computations={%region_11.11_spmd, %region_12.12_spmd} | conditional | flops 2699625728 | bytes 80468128 | solution.py:250
  274.5 4.3 fusion.42
  278.9 2.6 convolution_convert_fusion.9
  285.5 3.4 convolution_convert_fusion.3
  293.8 146.8 %reduce-scatter.10.cloned.1.call-done = bf16[256,512]{0,1:T(8,128)(2,1)} async-done(((bf16[2048,512]{0,1:T(8,128)(2,1)}), bf16[256,512]{0,1:T(8,128)(2,1)}) %reduce-scatter.10.cloned.1.call-update) | async-done | bytes 262160 | tf_op jit(solution)/shard_map/reduce_scatter | solution.py:268
  443.2 4.2 convolution_convert_fusion.2
  448.7 4.2 convolution_convert_fusion.1
  454.4 4.2 convolution_convert_fusion
  458.9 4.9 reduce-scatter.18.cloned.1.call-done
  463.8 24.9 %reduce-scatter.16.cloned.1.call-done = bf16[256,256]{1,0:T(8,128)(2,1)} async-done(((bf16[1024,256]{1,0:T(8,128)(2,1)}), bf16[256,256]{1,0:T(8,128)(2,1)}) %reduce-scatter.16.cloned.1.call-update) | async-done | bytes 131088 | tf_op jit(solution)/shard_map/reduce_scatter | solution.py:303
  488.7 34.4 %reduce-scatter.20.cloned.1.call-done = bf16[256,1024]{1,0:T(8,128)(2,1)} async-done(((bf16[1024,1024]{1,0:T(8,128)(2,1)}), bf16[256,1024]{1,0:T(8,128)(2,1)}) %reduce-scatter.20.cloned.1.call-update) | async-done | bytes 524304 | tf_op jit(solution)/shard_map/reduce_scatter | solution.py:309
  523.1 34.7 %reduce-scatter.12.cloned.1.call-done = bf16[256,1024]{1,0:T(8,128)(2,1)} async-done(((bf16[1024,1024]{1,0:T(8,128)(2,1)}), bf16[256,1024]{1,0:T(8,128)(2,1)}) %reduce-scatter.12.cloned.1.call-update) | async-done | bytes 524304 | tf_op jit(solution)/shard_map/reduce_scatter | solution.py:297
  557.9 27.9 %reduce-scatter.14.cloned.1.call-done = bf16[256,512]{1,0:T(8,128)(2,1)} async-done(((bf16[1024,512]{1,0:T(8,128)(2,1)}), bf16[256,512]{1,0:T(8,128)(2,1)}) %reduce-scatter.14.cloned.1.call-update) | async-done | bytes 262160 | tf_op jit(solution)/shard_map/reduce_scatter | solution.py:300
  585.8 57.6 %reduce-scatter.22.cloned.1.call-done = bf16[1024,704]{0,1:T(8,128)(2,1)} async-done(((bf16[1024,2816]{0,1:T(8,128)(2,1)}), bf16[1024,704]{0,1:T(8,128)(2,1)}) %reduce-scatter.22.cloned.1.call-update) | async-done | bytes 1441808 | tf_op jit(solution)/shard_map/reduce_scatter | solution.py:315
  643.4 57.3 %reduce-scatter.24.cloned.1.call-done = bf16[1024,704]{0,1:T(8,128)(2,1)} async-done(((bf16[1024,2816]{0,1:T(8,128)(2,1)}), bf16[1024,704]{0,1:T(8,128)(2,1)}) %reduce-scatter.24.cloned.1.call-update) | async-done | bytes 1441808 | tf_op jit(solution)/shard_map/reduce_scatter | solution.py:318
  700.6 57.5 %reduce-scatter.26.cloned.1.call-done = bf16[704,1024]{1,0:T(8,128)(2,1)} async-done(((bf16[2816,1024]{1,0:T(8,128)(2,1)}), bf16[704,1024]{1,0:T(8,128)(2,1)}) %reduce-scatter.26.cloned.1.call-update) | async-done | bytes 1441808 | tf_op jit(solution)/shard_map/reduce_scatter | solution.py:321
  762.4 5.6 fusion.53
  768.8 6.1 all-reduce.4
  775.0 22.1 %all-reduce.2 = (bf16[256]{0:T(256)(128)(2,1)S(1)}, bf16[256]{0:T(256)(128)(2,1)S(1)}) all-reduce(bf16[256]{0:T(256)(128)(2,1)S(1)} %dynamic-slice.1, bf16[256]{0:T(256)(128)(2,1)S(1)} %dynamic-slice.3), channel_id=1, replica_groups=mesh['ctx'=8,'fsdp'=4] {'ctx'}, use_global_device_ids=true, to_apply=%region_18.19 | all-reduce | flops 512 | bytes 2048 | tf_op jit(solution)/shard_map/psum | solution.py:326
  799.5 167.7 %all-reduce.7.cloned.1.call-done = (bf16[256,1024]{1,0:T(8,128)(2,1)}, bf16[256,512]{1,0:T(8,128)(2,1)}, bf16[256,256]{1,0:T(8,128)(2,1)}, bf16[256,256]{1,0:T(8...) async-done(((bf16[256,1024]{1,0:T(8,128)(2,1)}, bf16[256,512]{1,0:T(8,128)(2,1)}, ...) | async-done | bytes 5898256 | tf_op jit(solution)/shard_map/psum | solution.py:327
  967.2 3.4 convert_element_type.275
  (259 shorter events, 86.7 us)
Async XLA Ops:
  7.2 21.8 %all-gather.9.cloned.1.call-start = ((), (), s32[]{:S(2)}) async-start(), calls=%async_computation.9 | async-start | bytes 1310720 | tf_op jit(solution)/shard_map/all_gather | solution.py:76
  7.9 109.8 %all-gather.13.cloned.1.call-start = ((), (), s32[]{:S(2)}) async-start(), calls=%async_computation.11 | async-start | bytes 2621440 | tf_op jit(solution)/shard_map/all_gather | solution.py:75
  8.7 120.1 %all-gather.11.cloned.1.call-start = ((), (), s32[]{:S(2)}) async-start(), calls=%async_computation.10 | async-start | bytes 2359296 | tf_op jit(solution)/shard_map/all_gather | solution.py:157
  15.3 102.4 %copy-start.43 = (f32[4,1,256]{2,1,0:T(1,128)}, f32[4,1,256]{2,1,0:T(1,128)S(1)}, u32[]{:S(2)}) copy-start(f32[4,1,256]{2,1,0:T(1,128)S(1)} %convert_element_type.282) | copy-start | bytes 12292
  16.6 101.2 %copy-start.45 = (f32[256]{0:T(256)}, f32[256]{0:T(256)S(1)}, u32[]{:S(2)}) copy-start(f32[256]{0:T(256)S(1)} %add_rsqrt_fusion.1) | copy-start | bytes 3076
  29.0 4.5 copy-start.30
  29.0 34.9 %copy-start.47 = (bf16[256]{0:T(256)(128)(2,1)S(1)}, bf16[256]{0:T(256)(128)(2,1)}, u32[]{:S(2)}) copy-start(bf16[256]{0:T(256)(128)(2,1)} %param.30) | copy-start | bytes 1540
  31.7 124.6 %all-gather.15.cloned.1.call-start = ((), (), s32[]{:S(2)}) async-start(), calls=%async_computation.12 | async-start | bytes 2621440 | tf_op jit(solution)/shard_map/all_gather | solution.py:79
  32.3 146.0 %all-gather.17.cloned.1.call-start = ((), (), s32[]{:S(2)}) async-start(), calls=%async_computation.13 | async-start | bytes 7208960 | tf_op jit(solution)/shard_map/all_gather | solution.py:100
  32.9 190.2 %all-gather.19.cloned.1.call-start = ((), (), s32[]{:S(2)}) async-start(), calls=%async_computation.14 | async-start | bytes 7208960 | tf_op jit(solution)/shard_map/all_gather | solution.py:101
  33.5 407.1 %reduce-scatter.10.cloned.1.call-start = ((), (), s32[]{:S(2)}) async-start(), calls=%async_computation.15 | async-start | bytes 2359296 | tf_op jit(solution)/shard_map/reduce_scatter | solution.py:268
  33.5 29.7 %collective-permute-start = (bf16[704,1024]{1,0:T(8,128)(2,1)S(1)}, bf16[704,1024]{1,0:T(8,128)(2,1)S(1)}, u32[]{:S(2)}, u32[]{:S(2)}) collective-permute-start(bf16[704,1024]{1,0:T(8,128)(2,1)S(1)} %copy-done.30), channel_id=1, source_target_pairs={{0,1},{1,2},{2,3},{3,0},{4,5},{5,6},{6,7},{7,4},{8,9},{9,10},{10,1... | collective-permute-start | bytes 4325384 | tf_op jit(solution)/shard_map/ppermute | solution.py:95
  63.3 22.8 %copy-start.31 = (bf16[704,1024]{1,0:T(8,128)(2,1)}, bf16[704,1024]{1,0:T(8,128)(2,1)S(1)}, u32[]{:S(2)}) copy-start(bf16[704,1024]{1,0:T(8,128)(2,1)S(1)} %collective-permute-done) | copy-start | bytes 4325380
  63.3 19.3 %collective-permute-start.1 = (bf16[704,1024]{1,0:T(8,128)(2,1)S(1)}, bf16[704,1024]{1,0:T(8,128)(2,1)}, u32[]{:S(2)}, u32[]{:S(2)}) collective-permute-start(bf16[704,1024]{1,0:T(8,128)(2,1)S(1)} %collective-permute-done), channel_id=1, source_target_pairs={{0,1},{1,2},{2,3},{3,0},{4,5},{5,6},{6,7},{7,4},{8,9},{9,10},{10,1... | collective-permute-start | bytes 4325384 | tf_op jit(solution)/shard_map/ppermute | solution.py:95
  82.6 43.5 %collective-permute-start.2 = (bf16[704,1024]{1,0:T(8,128)(2,1)}, bf16[704,1024]{1,0:T(8,128)(2,1)}, u32[]{:S(2)}, u32[]{:S(2)}) collective-permute-start(bf16[704,1024]{1,0:T(8,128)(2,1)} %collective-permute-done.1), channel_id=1, source_target_pairs={{0,1},{1,2},{2,3},{3,0},{4,5},{5,6},{6,7},{7,4},{8,9},{9,10},{10,1... | collective-permute-start | bytes 4325384 | tf_op jit(solution)/shard_map/ppermute | solution.py:95
  86.1 18.9 %copy-start.40 = (bf16[256,256]{1,0:T(8,128)(2,1)S(1)}, bf16[256,256]{1,0:T(8,128)(2,1)}, u32[]{:S(2)}) copy-start(bf16[256,256]{1,0:T(8,128)(2,1)} %param.28) | copy-start | bytes 393220
  104.9 15.7 %copy-start.17 = (bf16[1024,256]{1,0:T(8,128)(2,1)}, bf16[1024,256]{1,0:T(8,128)(2,1)S(1)}, u32[]{:S(2)}) copy-start(bf16[1024,256]{1,0:T(8,128)(2,1)S(1)} %all_gather.34) | copy-start | bytes 1572868
  112.5 5.3 copy-start.6
  151.8 4.1 copy-start.18
  156.3 2.7 copy-start.16
  223.1 4.5 copy-start.24
  223.1 13.3 %slice-start = ((s8[5767168]{0:T(1024)(128)(4,1)}), s8[4194304]{0:T(1024)(128)(4,1)S(1)}, s32[]{:S(2)}) async-start(s8[5767168]{0:T(1024)(128)(4,1)} %bitcast.218), calls=%async_computation.25 | async-start | bytes 8388608
  223.1 15.0 %slice-start.2 = ((s8[5767168]{0:T(1024)(128)(4,1)}), s8[4194304]{0:T(1024)(128)(4,1)S(1)}, s32[]{:S(2)}) async-start(s8[5767168]{0:T(1024)(128)(4,1)} %bitcast.220), calls=%async_computation.27 | async-start | bytes 8388608
  227.6 8.8 slice-start.1
  227.7 10.5 %slice-start.3 = ((s8[5767168]{0:T(1024)(128)(4,1)}), s8[1572864]{0:T(1024)(128)(4,1)S(1)}, s32[]{:S(2)}) async-start(s8[5767168]{0:T(1024)(128)(4,1)} %bitcast.220), calls=%async_computation.28 | async-start | bytes 3145728
  247.9 3.6 copy-start.13
  274.5 4.3 copy-start.5
  278.8 185.0 %reduce-scatter.18.cloned.1.call-start = ((), (), s32[]{:S(2)}) async-start(), calls=%async_computation.19 | async-start | bytes 655360 | tf_op jit(solution)/shard_map/reduce_scatter | solution.py:306
  281.5 207.2 %reduce-scatter.16.cloned.1.call-start = ((), (), s32[]{:S(2)}) async-start(), calls=%async_computation.18 | async-start | bytes 655360 | tf_op jit(solution)/shard_map/reduce_scatter | solution.py:303
  285.4 237.7 %reduce-scatter.20.cloned.1.call-start = ((), (), s32[]{:S(2)}) async-start(), calls=%async_computation.20 | async-start | bytes 2621440 | tf_op jit(solution)/shard_map/reduce_scatter | solution.py:309
  288.9 2.7 copy-start.44
  288.9 2.7 copy-start.46
  288.9 269.0 %reduce-scatter.12.cloned.1.call-start = ((), (), s32[]{:S(2)}) async-start(), calls=%async_computation.16 | async-start | bytes 2621440 | tf_op jit(solution)/shard_map/reduce_scatter | solution.py:297
  293.7 149.5 %copy-start.29 = (bf16[256,2816]{1,0:T(8,128)(2,1)S(1)}, bf16[256,2816]{1,0:T(8,128)(2,1)}, u32[]{:S(2)}) copy-start(bf16[256,2816]{1,0:T(8,128)(2,1)} %copy-done.28) | copy-start | bytes 4325380
  293.8 292.0 %reduce-scatter.14.cloned.1.call-start = ((), (), s32[]{:S(2)}) async-start(), calls=%async_computation.17 | async-start | bytes 1310720 | tf_op jit(solution)/shard_map/reduce_scatter | solution.py:300
  443.1 200.2 %reduce-scatter.22.cloned.1.call-start = ((), (), s32[]{:S(2)}) async-start(), calls=%async_computation.21 | async-start | bytes 7208960 | tf_op jit(solution)/shard_map/reduce_scatter | solution.py:315
  447.4 253.2 %reduce-scatter.24.cloned.1.call-start = ((), (), s32[]{:S(2)}) async-start(), calls=%async_computation.22 | async-start | bytes 7208960 | tf_op jit(solution)/shard_map/reduce_scatter | solution.py:318
  452.9 305.2 %reduce-scatter.26.cloned.1.call-start = ((), (), s32[]{:S(2)}) async-start(), calls=%async_computation.23 | async-start | bytes 7208960 | tf_op jit(solution)/shard_map/reduce_scatter | solution.py:321
  458.6 508.6 %all-reduce.7.cloned.1.call-start = ((), (), s32[]{:S(2)}) async-start(), calls=%async_computation.24 | async-start | bytes 11796480 | tf_op jit(solution)/shard_map/psum | solution.py:327
  758.2 4.2 copy-start.11
  762.4 5.6 copy-start.34
  762.4 5.6 copy-start.35
  768.0 30.2 %copy-start.8 = (f32[256,1024]{1,0:T(8,128)S(1)}, f32[256,1024]{1,0:T(8,128)}, u32[]{:S(2)}) copy-start(f32[256,1024]{1,0:T(8,128)} %copy-done.7) | copy-start | bytes 3145732
  967.2 3.4 copy-start.33
  972.5 3.0 copy-start.36
  972.5 4.1 copy-start.38
  974.5 3.0 copy-start.42
  974.5 3.8 copy-start.41
  (24 other events, 40.0 us)
Sparse Core Ops, SparseCore 0:
  9.6 19.4 all-gather.8
  30.6 28.2 all-gather.12
  61.6 49.2 all-gather.10
  112.3 21.0 all-gather.14
  134.8 43.3 all-gather.16
  179.7 43.3 all-gather.18
  278.9 161.6 reduce-scatter.9
  443.1 20.6 reduce-scatter.17
  467.0 21.6 reduce-scatter.15
  491.7 31.4 reduce-scatter.19
  526.4 31.4 reduce-scatter.11
  560.8 24.8 reduce-scatter.13
  588.5 54.8 reduce-scatter.21
  645.8 54.8 reduce-scatter.23
  703.2 54.8 reduce-scatter.25
  762.6 204.5 all-reduce.6
